TPU v7x, 128 devices: a whole 4x4x4 slice. The times are simulated.
128 devices in a mesh: row: 16 (over y_lo, z, core), col: 8 (over x, y_hi).
Axes of the slice: x: 4, y: 4 (y_hi: 2, y_lo: 2; y = y_hi * 2 + y_lo), z: 4, core: 2. Of those that a mesh axis runs over, the one named last changes fastest.
Arguments:
- hidden_in: bfloat16 [8192, 2048], P('row'), may hold values from -6 to 6
- gain_attn: float32 [2048], replicated, may hold values from 0.1 to 1.9
- gain_mlp: float32 [2048], replicated, may hold values from 0.1 to 1.9
- w_qkv: bfloat16 [2048, 3, 2048], P('row', None, 'col'), may hold values from -0.25 to 0.25
- w_up: bfloat16 [2048, 8192], P('row', 'col'), may hold values from -0.25 to 0.25
- w_out: bfloat16 [2048, 2048], P('col', 'row'), may hold values from -0.125 to 0.125
- w_down: bfloat16 [8192, 2048], P('col', 'row'), may hold values from -0.0625 to 0.0625
- prefix_cache: bfloat16 [128, 128, 2, 2048], P('row', None, None, 'col'), may hold values from -136 to 136, as said below
- suffix_lengths: int32 [64], replicated, may hold values from 1 to 512, 8192 in all
- cached_lengths: int32 [64], replicated, may hold values from 1 to 8192, as said below
- request_group: int32 [64], replicated, may hold values from 0 to 1
- page_table: int32 [128], replicated, may hold values from 0 to 127, each once
Outputs:
- hidden_out: bfloat16 [8192, 2048], P('row', 'col')
- suffix_keys: bfloat16 [8192, 2048], P('row', 'col')
- suffix_values: bfloat16 [8192, 2048], P('row', 'col')
Inputs may be any that keep to these rules, and one draw needn't show every extreme that they name: `suffix_lengths`: the lengths sum to 8192; some request has exactly 512 tokens. `cached_lengths`: some request reuses all 8192 tokens of its prefix. `page_table`: each slot appears once; slot s is held by index s // 8 of row. `prefix_cache`: keys and values of the prefix pages.
All inputs are finite; a program needn't handle non-finite values.
Results may differ from a plain program's by a relative error of at most 0.02.
Values may be sent and summed in bfloat16 or wider, within the bound.
A program may use at most 128 MiB of HBM per device.

v0:
```python
import math

import jax
import jax.numpy as jnp
from jax import lax
from jax.sharding import PartitionSpec as P

HD = 256
ROT = 64
PAGE = 128
GROUPS = 2


very_low = -1e30
norm_epsilon = 1e-05


def from_behind(block, axis, distance):
    devices = range(lax.axis_size(axis))
    route = [(i - distance, i) for i in devices if i - distance in devices]
    return lax.ppermute(block, axis, route)


def layer_normalize(values):
    floats = values.astype(jnp.float32)
    average = jnp.mean(floats, -1, keepdims=True)
    centered = floats - average
    spread = jnp.mean(centered * centered, -1, keepdims=True)
    return centered * lax.rsqrt(spread + norm_epsilon)


def rotary(vectors, position):
    half_rot = ROT // 2
    exponent = jnp.arange(half_rot, dtype=jnp.float32) * (2.0 / ROT)
    frequency = 10000.0 ** (-exponent)
    angles = position.astype(jnp.float32)[:, None] * frequency[None, :]
    cosine = jnp.concatenate([jnp.cos(angles), jnp.cos(angles)], 1)[:, None, :]
    sine = jnp.concatenate([jnp.sin(angles), jnp.sin(angles)], 1)[:, None, :]
    rotated = vectors[..., :ROT]
    turned = jnp.concatenate([-rotated[..., half_rot:], rotated[..., :half_rot]], -1)
    return jnp.concatenate([rotated * cosine + turned * sine, vectors[..., ROT:]], -1)


def token_table(suffix_lengths, cached_lengths, request_group, count):
    starts = jnp.cumsum(suffix_lengths, dtype=jnp.int32) - suffix_lengths
    token_ids = jnp.arange(count, dtype=jnp.int32)
    request = (
        jnp.sum((starts[None, :] <= token_ids[:, None]).astype(jnp.int32), 1, dtype=jnp.int32) - 1
    )
    onehot = (
        request[:, None] == jnp.arange(suffix_lengths.shape[0], dtype=jnp.int32)[None, :]
    ).astype(jnp.int32)
    begin = jnp.sum(onehot * starts[None, :], 1, dtype=jnp.int32)
    limit = jnp.sum(onehot * cached_lengths[None, :], 1, dtype=jnp.int32)
    group_of = jnp.sum(onehot * request_group[None, :], 1, dtype=jnp.int32)
    return (request, limit + token_ids - begin, group_of, limit)


def partial_softmax(scores, visible, value_block):
    allowed = visible[None, :, :]
    peak = jnp.max(jnp.where(allowed, scores, very_low), -1)
    weights = jnp.where(allowed, jnp.exp(scores - peak[..., None]), 0.0)
    total = jnp.sum(weights, -1)
    mixed = jnp.einsum(
        "hqk,khe->qhe",
        weights.astype(jnp.bfloat16),
        value_block,
        preferred_element_type=jnp.float32,
    )
    return (peak, total, mixed)


def combine(earlier, later):
    peak = jnp.maximum(earlier[0], later[0])
    scale_one = jnp.exp(earlier[0] - peak)
    scale_two = jnp.exp(later[0] - peak)
    total = earlier[1] * scale_one + later[1] * scale_two
    mixed = earlier[2] * scale_one.T[:, :, None] + later[2] * scale_two.T[:, :, None]
    return (peak, total, mixed)


def prefix_fold(running, cache_rows, query_block, query_group, query_limit, page_table):
    count = cache_rows.shape[0]
    stride = math.gcd(count, 8)
    heads_here = query_block.shape[1]
    per_prefix = page_table.shape[0] // GROUPS
    table_index = jnp.arange(page_table.shape[0], dtype=jnp.int32)

    def advance(turn_index, inner):
        block_rows = lax.dynamic_slice_in_dim(cache_rows, turn_index * stride, stride, 0)
        slots = turn_index * stride + jnp.arange(stride, dtype=jnp.int32)
        logical = jnp.sum(
            table_index[None, :] * (page_table[None, :] == slots[:, None]).astype(jnp.int32),
            1,
            dtype=jnp.int32,
        )
        key_group = jnp.repeat(logical // per_prefix, PAGE)
        key_position = (
            (logical % per_prefix)[:, None] * PAGE + jnp.arange(PAGE, dtype=jnp.int32)[None, :]
        ).reshape(-1)
        key_block = block_rows[:, :, 0].reshape(stride * PAGE, heads_here, HD)
        value_block = block_rows[:, :, 1].reshape(stride * PAGE, heads_here, HD)
        visible = (key_group[None, :] == query_group[:, None]) & (
            key_position[None, :] < query_limit[:, None]
        )
        scores = jnp.einsum(
            "qhe,khe->hqk", query_block, key_block, preferred_element_type=jnp.float32
        )
        return combine(inner, partial_softmax(scores, visible, value_block))

    return lax.fori_loop(0, count // stride, advance, running)


def body(
    hidden_in,
    gain_attn,
    gain_mlp,
    w_qkv,
    w_up,
    w_out,
    w_down,
    prefix_cache,
    suffix_lengths,
    cached_lengths,
    request_group,
    page_table,
):
    row_count = hidden_in.shape[0]
    model_width = hidden_in.shape[1]
    row_total = lax.axis_size("row")
    col_total = lax.axis_size("col")
    row_place = lax.axis_index("row")
    col_place = lax.axis_index("col")
    head_width = w_qkv.shape[2]
    heads_here = head_width // HD
    normed = layer_normalize(hidden_in)
    attn_in = (normed * gain_attn).astype(jnp.bfloat16)
    mlp_in = (normed * gain_mlp).astype(jnp.bfloat16)
    pieces = (
        lax.all_gather(w_qkv, "row", axis=0, tiled=True),
        lax.all_gather(w_up, "row", axis=0, tiled=True),
    )
    projected = jnp.einsum("td,dkh->tkh", attn_in, pieces[0], preferred_element_type=jnp.float32)
    up_sum = jnp.dot(mlp_in, pieces[1], preferred_element_type=jnp.float32)
    token_total = row_total * row_count
    request_all, position_all, group_all, limit_all = token_table(
        suffix_lengths, cached_lengths, request_group, token_total
    )
    first_row = row_place * row_count
    local_request = lax.dynamic_slice_in_dim(request_all, first_row, row_count, 0)
    local_position = lax.dynamic_slice_in_dim(position_all, first_row, row_count, 0)
    local_group = lax.dynamic_slice_in_dim(group_all, first_row, row_count, 0)
    local_limit = lax.dynamic_slice_in_dim(limit_all, first_row, row_count, 0)
    projected = projected.reshape(row_count, 3, heads_here, HD)
    queries = (rotary(projected[:, 0], local_position) * HD ** (-0.5)).astype(jnp.bfloat16)
    keys_flat = (
        rotary(projected[:, 1], local_position).astype(jnp.bfloat16).reshape(row_count, head_width)
    )
    values_flat = projected[:, 2].astype(jnp.bfloat16).reshape(row_count, head_width)
    pair_rows = jnp.stack([keys_flat, values_flat], 1)
    previous = from_behind(pair_rows, "row", 1)
    window = jnp.concatenate([previous, pair_rows], 0)
    window_ids = first_row - row_count + jnp.arange(2 * row_count, dtype=jnp.int32)
    padded_request = jnp.concatenate([jnp.full((row_count,), -1, jnp.int32), request_all], 0)
    window_request = lax.dynamic_slice_in_dim(padded_request, first_row, 2 * row_count, 0)
    token_ids = first_row + jnp.arange(row_count, dtype=jnp.int32)
    visible = (window_request[None, :] == local_request[:, None]) & (
        window_ids[None, :] <= token_ids[:, None]
    )
    window_keys = window[:, 0].reshape(2 * row_count, heads_here, HD)
    window_values = window[:, 1].reshape(2 * row_count, heads_here, HD)
    scores = jnp.einsum("qhe,khe->hqk", queries, window_keys, preferred_element_type=jnp.float32)
    suffix_state = partial_softmax(scores, visible, window_values)
    start_state = (
        jnp.full((heads_here, row_count), very_low, jnp.float32),
        jnp.zeros((heads_here, row_count), jnp.float32),
        jnp.zeros((row_count, heads_here, HD), jnp.float32),
    )
    prefix_state = prefix_fold(
        start_state,
        lax.all_gather(prefix_cache, "row", axis=0, tiled=True),
        queries,
        local_group,
        local_limit,
        page_table,
    )
    final = combine(prefix_state, suffix_state)
    attention = (
        (final[2] / final[1].T[:, :, None]).astype(jnp.bfloat16).reshape(row_count, head_width)
    )
    activated = jax.nn.gelu(up_sum, approximate=False).astype(jnp.bfloat16)
    pieces = (
        lax.all_gather(w_out, "row", axis=1, tiled=True),
        lax.all_gather(w_down, "row", axis=1, tiled=True),
    )
    contribution = jnp.dot(attention, pieces[0], preferred_element_type=jnp.float32) + jnp.dot(
        activated, pieces[1], preferred_element_type=jnp.float32
    )
    summed = lax.psum_scatter(
        contribution.astype(jnp.bfloat16), "col", scatter_dimension=1, tiled=True
    ).astype(jnp.float32)
    share = model_width // col_total
    residual = lax.dynamic_slice_in_dim(hidden_in, col_place * share, share, 1).astype(jnp.float32)
    return ((residual + summed).astype(jnp.bfloat16), keys_flat, values_flat)


def solution(mesh):
    in_specs = (
        P("row", None),
        P(),
        P(),
        P("row", None, "col"),
        P("row", "col"),
        P("col", "row"),
        P("col", "row"),
        P("row", None, None, "col"),
        P(),
        P(),
        P(),
        P(),
    )
    out_specs = (P("row", "col"), P("row", "col"), P("row", "col"))
    return jax.shard_map(body, mesh=mesh, in_specs=in_specs, out_specs=out_specs, check_vma=False)
```

profile of v0, /device:TPU:28, one launch (start us, length us, event | category | flops | bytes accessed | tf_op | source)
XLA Modules:
  0.0 415.6 jit_solution(5425519971744105264)
XLA Ops:
  7.2 1.7 copy.32
  10.5 2.4 copy.31
  17.3 36.3 %all-gather.8.cloned.1.call-done = bf16[2048,3,256]{0,2,1:T(8,128)(2,1)} async-done(((bf16[128,3,256]{0,2,1:T(8,128)(2,1)}), bf16[2048,3,256]{0,2,1:T(8,128)(2,1)}) %all-gather.8.cloned.1.call-update) | async-done | bytes 3145744 | tf_op jit(solution)/shard_map/all_gather | solution.py:140
  53.6 3.9 fusion.37
  60.0 2.3 collective-permute-start
  66.3 15.7 %collective-permute-done = bf16[512,2,256]{0,2,1:T(8,128)(2,1)} collective-permute-done((bf16[512,2,256]{0,2,1:T(8,128)(2,1)}, bf16[512,2,256]{0,2,1:T(8,128)(2,1)}, u32[]{:S(2)}, u32[]{:S(2)}) %collective-permute-start) | collective-permute-done | bytes 524320 | tf_op jit(solution)/shard_map/ppermute | solution.py:21
  84.3 1.3 copy-done.1
  86.3 8.7 %all-gather.12.cloned.1.call-done = bf16[2048,1024]{1,0:T(8,128)(2,1)} async-done(((bf16[128,1024]{1,0:T(8,128)(2,1)}), bf16[2048,1024]{1,0:T(8,128)(2,1)}) %all-gather.12.cloned.1.call-update) | async-done | bytes 4194320 | tf_op jit(solution)/shard_map/all_gather | solution.py:141
  95.0 46.8 %all-gather.14.cloned.1.call-done = bf16[1024,2048]{1,0:T(8,128)(2,1)} async-done(((bf16[1024,128]{1,0:T(8,128)(2,1)}), bf16[1024,2048]{1,0:T(8,128)(2,1)}) %all-gather.14.cloned.1.call-update) | async-done | bytes 4194320 | tf_op jit(solution)/shard_map/all_gather | solution.py:194
  141.8 14.4 %fusion.55 = f32[512,2048]{1,0:T(8,128)} fusion(bf16[1024,2048]{1,0:T(8,128)(2,1)} %all-gather.14.cloned.1.call-done, bf16[2048,1024]{1,0:T(8,128)(2,1)} %all-gather.12.cloned.1.call-done, bf16[512,2048]{1,0:T(8,128)(2,1)S(1)} %copy-done, f32[2048]{0:T(1024)S(1)} %copy-done.20, f32[512]{0:T(512)S(1)} %copy-done.15, f32[512]{0:T(512)S(1)} %copy-done.13), kind=kOutput, calls=%fused_computation.89 | convolution fusion | flops 4334288896 | bytes 14692352 | tf_op jit(solution)/shard_map/dot_general | solution.py:196
  156.2 79.2 %all-gather.6.cloned.1.call-done = bf16[128,128,2,256]{3,1,0,2:T(8,128)(2,1)} async-done(((bf16[8,128,2,256]{3,1,0,2:T(8,128)(2,1)}), bf16[128,128,2,256]{3,1,0,2:T(8,128)(2,1)}) %all-gather.6.cloned.1.call-update) | async-done | bytes 16777232 | tf_op jit(solution)/shard_map/all_gather | solution.py:181
  235.4 91.3 %while.20 = (s32[]{:T(128)}, f32[1,512]{1,0:T(1,128)S(1)}, f32[1,512]{1,0:T(1,128)S(1)}, f32[512,1,256]{0,2,1:T(8,128)}, s32[128]{0:T(128)S(1)}, /*index=5*/s32[...) while((s32[]{:T(128)}, f32[1,512]{1,0:T(1,128)S(1)}, ...), condition=%wide.region_11.12_spmd.clone, body=%wide.region_7.0_spmd.clone.sunk | while | flops 546315392 | bytes 11871218 | solution.py:111
  238.4 1.7 fusion.186
  243.2 2.7 fusion.186
  248.9 2.7 fusion.186
  254.7 2.7 fusion.186
  257.4 1.3 constant_dynamic-slice_fusion.3
  260.5 2.7 fusion.186
  266.3 2.7 fusion.186
  272.0 2.7 fusion.186
  277.8 2.7 fusion.186
  283.6 2.7 fusion.186
  289.3 2.7 fusion.186
  295.1 2.7 fusion.186
  300.9 2.7 fusion.186
  306.6 2.7 fusion.186
  312.4 2.7 fusion.186
  318.2 2.7 fusion.186
  323.9 2.7 fusion.186
  326.7 6.3 %add_convert_fusion = bf16[512,2048]{1,0:T(8,128)(2,1)} fusion(f32[512,2048]{1,0:T(8,128)} %fusion.55, bf16[256,2048]{1,0:T(8,128)(2,1)} %all-gather.10.cloned.1.call-done, f32[512,1024]{1,0:T(8,128)} %copy-done.1, f32[512]{0:T(512)S(1)} %get-tuple-element.373, s32[1024]{0:T(1024)S(1)} %get-tuple-element.378, s32[1024]{0:T(1024)S(1)} %get-tuple-element.377, ...), kind=kOutput, calls=%fused_computation.51 | convolution fusion | flops 811204608 | bytes 10506240 | tf_op jit(solution)/shard_map/dot_general | solution.py:196
  334.8 72.2 %reduce-scatter.2.cloned.1.call-done = bf16[512,256]{1,0:T(8,128)(2,1)} async-done(((bf16[512,2048]{1,0:T(8,128)(2,1)}), bf16[512,256]{1,0:T(8,128)(2,1)}) %reduce-scatter.2.cloned.1.call-update) | async-done | bytes 262160 | tf_op jit(solution)/shard_map/reduce_scatter | solution.py:199
  406.9 1.8 add_convert_fusion.1
  (251 shorter events, 64.2 us)
Async XLA Ops:
  7.2 6.4 %copy-start.16 = (s32[64]{0:T(128)S(1)}, s32[64]{0:T(128)}, u32[]{:S(2)}) copy-start(s32[64]{0:T(128)} %param.22) | copy-start | bytes 772
  7.2 46.4 %all-gather.8.cloned.1.call-start = ((), (), s32[]{:S(2)}) async-start(), calls=%async_computation.2 | async-start | bytes 3342336 | tf_op jit(solution)/shard_map/all_gather | solution.py:140
  9.0 5.3 %copy-start = (bf16[512,2048]{1,0:T(8,128)(2,1)S(1)}, bf16[512,2048]{1,0:T(8,128)(2,1)}, u32[]{:S(2)}) copy-start(bf16[512,2048]{1,0:T(8,128)(2,1)} %param.14) | copy-start | bytes 6291460
  9.0 86.0 %all-gather.12.cloned.1.call-start = ((), (), s32[]{:S(2)}) async-start(), calls=%async_computation.4 | async-start | bytes 4456448 | tf_op jit(solution)/shard_map/all_gather | solution.py:141
  9.7 132.1 %all-gather.14.cloned.1.call-start = ((), (), s32[]{:S(2)}) async-start(), calls=%async_computation.5 | async-start | bytes 4456448 | tf_op jit(solution)/shard_map/all_gather | solution.py:194
  10.5 224.9 %all-gather.6.cloned.1.call-start = ((), (), s32[]{:S(2)}) async-start(), calls=%async_computation.1 | async-start | bytes 17825792 | tf_op jit(solution)/shard_map/all_gather | solution.py:181
  12.9 313.8 %all-gather.10.cloned.1.call-start = ((), (), s32[]{:S(2)}) async-start(), calls=%async_computation.3 | async-start | bytes 1114112 | tf_op jit(solution)/shard_map/all_gather | solution.py:193
  13.5 393.4 %reduce-scatter.2.cloned.1.call-start = ((), (), s32[]{:S(2)}) async-start(), calls=%async_computation.6 | async-start | bytes 2359296 | tf_op jit(solution)/shard_map/reduce_scatter | solution.py:199
  14.3 39.3 %copy-start.19 = (f32[2048]{0:T(1024)S(1)}, f32[2048]{0:T(1024)}, u32[]{:S(2)}) copy-start(f32[2048]{0:T(1024)} %param.15) | copy-start | bytes 24580
  14.7 42.8 %copy-start.12 = (f32[512]{0:T(512)}, f32[512]{0:T(512)S(1)}, u32[]{:S(2)}) copy-start(f32[512]{0:T(512)S(1)} %broadcast_multiply_fusion) | copy-start | bytes 6148
  15.4 42.1 %copy-start.14 = (f32[512]{0:T(512)}, f32[512]{0:T(512)S(1)}, u32[]{:S(2)}) copy-start(f32[512]{0:T(512)S(1)} %add_rsqrt_fusion) | copy-start | bytes 6148
  60.0 22.0 %collective-permute-start = (bf16[512,2,256]{0,2,1:T(8,128)(2,1)}, bf16[512,2,256]{0,2,1:T(8,128)(2,1)}, u32[]{:S(2)}, u32[]{:S(2)}) collective-permute-start(bf16[512,2,256]{0,2,1:T(8,128)(2,1)} %pad_maximum_fusion), channel_id=1, source_target_pairs={{0,8},{8,16},{16,24},{24,32},{32,40},{40,48},{48,56},{56,64},{64,7... | collective-permute-start | bytes 1572872 | tf_op jit(solution)/shard_map/ppermute | solution.py:21
  63.6 19.6 %copy-start.10 = (s32[512]{0:T(512)S(1)}, s32[512]{0:T(512)}, u32[]{:S(2)}) copy-start(s32[512]{0:T(512)} %iota_add_fusion.2) | copy-start | bytes 6148
  63.6 19.6 %copy-start.11 = (s32[512]{0:T(512)S(1)}, s32[512]{0:T(512)}, u32[]{:S(2)}) copy-start(s32[512]{0:T(512)} %dynamic_slice.33) | copy-start | bytes 6148
  64.4 18.8 %copy-start.5 = (f32[512,1,64]{0,2,1:T(8,128)S(1)}, f32[512,1,64]{0,2,1:T(8,128)}, u32[]{:S(2)}) copy-start(f32[512,1,64]{0,2,1:T(8,128)} %get-tuple-element.369) | copy-start | bytes 393220
  66.3 17.0 %copy-start.6 = (f32[512,192]{0,1:T(8,128)S(1)}, f32[512,192]{0,1:T(8,128)}, u32[]{:S(2)}) copy-start(f32[512,192]{0,1:T(8,128)} %get-tuple-element.364) | copy-start | bytes 1179652
  84.2 57.6 %copy-start.13 = (f32[512]{0:T(512)S(1)}, f32[512]{0:T(512)}, u32[]{:S(2)}) copy-start(f32[512]{0:T(512)} %copy-done.12) | copy-start | bytes 6148
  84.2 57.6 %copy-start.15 = (f32[512]{0:T(512)S(1)}, f32[512]{0:T(512)}, u32[]{:S(2)}) copy-start(f32[512]{0:T(512)} %copy-done.14) | copy-start | bytes 6148
  84.2 57.6 %copy-start.20 = (f32[2048]{0:T(1024)S(1)}, f32[2048]{0:T(1024)}, u32[]{:S(2)}) copy-start(f32[2048]{0:T(1024)} %param.16) | copy-start | bytes 24580
  86.3 149.0 %copy-start.21 = (s32[128]{0:T(128)S(1)}, s32[128]{0:T(128)}, u32[]{:S(2)}) copy-start(s32[128]{0:T(128)} %param.25) | copy-start | bytes 1540
  235.4 1.6 copy-start.7
  240.1 1.6 copy-start.7
  245.9 1.6 copy-start.7
  251.6 1.6 copy-start.7
  257.4 1.6 copy-start.7
  263.2 1.6 copy-start.7
  269.0 1.6 copy-start.7
  274.7 1.6 copy-start.7
  280.5 1.6 copy-start.7
  286.3 1.6 copy-start.7
  292.0 1.6 copy-start.7
  297.8 1.6 copy-start.7
  (12 other events, 15.2 us)
Sparse Core Ops, SparseCore 0:
  10.2 43.3 all-gather.7
  55.3 39.6 all-gather.11
  96.6 45.1 all-gather.13
  143.3 91.9 all-gather.5
  236.8 35.1 all-gather.9
  333.1 73.7 reduce-scatter.1
where the time goes:
time: 420 us; the launch traced here: 416 us
  waiting for transfers between devices  261 us (62%)
  matrix products  76.7 us (18%)
  local copies, waits for them, and re-layouts  31.9 us (8%)
  other arithmetic  28.9 us (7%)
  between operations  14.4 us (3%)
    all_gather x1, waiting for transfers between devices, body(): lax.all_gather(prefix_cache, 'row', axis=0, tiled=True)  79.2 us
    reduce_scatter x1, waiting for transfers between devices, body(): lax.psum_scatter(contribution.astype(jnp.bfloat16), 'col', scatter_dimens...  72.2 us
    all_gather x1, waiting for transfers between devices, body(): lax.all_gather(w_down, 'row', axis=1, tiled=True)  46.8 us
    dot_general x16, matrix products, partial_softmax(): jnp.einsum('hqk,khe->qhe', weights.astype(jnp.bfloat16), value_block, pre...  42.4 us
    all_gather x1, waiting for transfers between devices, body(): lax.all_gather(w_qkv, 'row', axis=0, tiled=True)  36.3 us
    slice x16, local copies, waits for them, and re-layouts, advance(): value_block = block_rows[:, :, 1].reshape(stride * PAGE, heads_here, HD)  21 us
    ppermute x1, waiting for transfers between devices, from_behind(): return lax.ppermute(block, axis, route)  15.7 us
    dot_general x1, matrix products, body(): jnp.dot(activated, pieces[1], preferred_element_type=jnp.float32)  14.4 us
  transfers between devices with their start and end apart: 7, of which 6 were waited for; matrix products, arithmetic and copies ran while one was open for 30% of the time, Pallas kernels for 0%

commit v1 on v0

--- a/solution.py
+++ b/solution.py
@@ -136,12 +136,13 @@
     normed = layer_normalize(hidden_in)
     attn_in = (normed * gain_attn).astype(jnp.bfloat16)
     mlp_in = (normed * gain_mlp).astype(jnp.bfloat16)
-    pieces = (
-        lax.all_gather(w_qkv, "row", axis=0, tiled=True),
-        lax.all_gather(w_up, "row", axis=0, tiled=True),
-    )
-    projected = jnp.einsum("td,dkh->tkh", attn_in, pieces[0], preferred_element_type=jnp.float32)
-    up_sum = jnp.dot(mlp_in, pieces[1], preferred_element_type=jnp.float32)
+    rows_here = w_qkv.shape[0]
+    qkv_columns = 3 * head_width
+    joined = jnp.concatenate([w_qkv.reshape(rows_here, qkv_columns), w_up], 1)
+    joined = lax.all_gather(joined, "row", axis=0, tiled=True)
+    qkv_all = joined[:, :qkv_columns].reshape(model_width, 3, head_width)
+    projected = jnp.einsum("td,dkh->tkh", attn_in, qkv_all, preferred_element_type=jnp.float32)
+    up_sum = jnp.dot(mlp_in, joined[:, qkv_columns:], preferred_element_type=jnp.float32)
     token_total = row_total * row_count
     request_all, position_all, group_all, limit_all = token_table(
         suffix_lengths, cached_lengths, request_group, token_total
@@ -189,13 +190,12 @@
         (final[2] / final[1].T[:, :, None]).astype(jnp.bfloat16).reshape(row_count, head_width)
     )
     activated = jax.nn.gelu(up_sum, approximate=False).astype(jnp.bfloat16)
-    pieces = (
-        lax.all_gather(w_out, "row", axis=1, tiled=True),
-        lax.all_gather(w_down, "row", axis=1, tiled=True),
-    )
-    contribution = jnp.dot(attention, pieces[0], preferred_element_type=jnp.float32) + jnp.dot(
-        activated, pieces[1], preferred_element_type=jnp.float32
-    )
+    out_rows = w_out.shape[0]
+    joined = jnp.concatenate([w_out.T, w_down.T], 1)
+    joined = lax.all_gather(joined, "row", axis=0, tiled=True)
+    contribution = jnp.einsum(
+        "th,dh->td", attention, joined[:, :out_rows], preferred_element_type=jnp.float32
+    ) + jnp.einsum("tf,df->td", activated, joined[:, out_rows:], preferred_element_type=jnp.float32)
     summed = lax.psum_scatter(
         contribution.astype(jnp.bfloat16), "col", scatter_dimension=1, tiled=True
     ).astype(jnp.float32)

time: 420 us -> 392 us (0.933)
  waiting for transfers between devices: 261 us -> 229 us
    ppermute x1, waiting for transfers between devices: 15.7 us -> 0.01 us  [from_behind(): return lax.ppermute(block, axis, route)]
    all_gather x4 -> x2, waiting for transfers between devices: 91.8 us -> 82.6 us  [body(): joined = lax.all_gather(joined, 'row', axis=0, tiled=True)]
    slice x0 -> x3, local copies, waits for them, and re-layouts: none -> 4.9 us  [body(): qkv_all = joined[:, :qkv_columns].reshape(model_width, 3, head_width)]
    all_gather x1, waiting for transfers between devices: 79.2 us -> 74.4 us  [body(): lax.all_gather(prefix_cache, 'row', axis=0, tiled=True)]
  transfers between devices with their start and end apart: 7 -> 5, of which waited for: 6 -> 4; matrix products, arithmetic and copies ran while one was open for 30% -> 9% of each run, Pallas kernels for 0% -> 0%
where the time goes in v1:
time: 392 us; the launch traced here: 387 us
  waiting for transfers between devices  229 us (58%)
  matrix products  77.4 us (20%)
  local copies, waits for them, and re-layouts  33.8 us (9%)
  other arithmetic  30 us (8%)
  between operations  14.1 us (4%)
    all_gather x2, waiting for transfers between devices, body(): joined = lax.all_gather(joined, 'row', axis=0, tiled=True)  82.6 us
    all_gather x1, waiting for transfers between devices, body(): lax.all_gather(prefix_cache, 'row', axis=0, tiled=True)  74.4 us
    reduce_scatter x1, waiting for transfers between devices, body(): lax.psum_scatter(contribution.astype(jnp.bfloat16), 'col', scatter_dimens...  72.1 us
    dot_general x16, matrix products, partial_softmax(): jnp.einsum('hqk,khe->qhe', weights.astype(jnp.bfloat16), value_block, pre...  42.5 us
    slice x16, local copies, waits for them, and re-layouts, advance(): value_block = block_rows[:, :, 1].reshape(stride * PAGE, heads_here, HD)  21 us
    dot_general x1, matrix products, body(): jnp.einsum('tf,df->td', activated, joined[:, out_rows:], preferred_elemen...  14.3 us
    reduce_sum x17, other arithmetic, partial_softmax(): total = jnp.sum(weights, -1)  14.2 us
    dot_general x16, matrix products, advance(): jnp.einsum('qhe,khe->hqk', query_block, key_block, preferred_element_type...  9.16 us
  transfers between devices with their start and end apart: 5, of which 4 were waited for; matrix products, arithmetic and copies ran while one was open for 9% of the time, Pallas kernels for 0%

profile of v1, /device:TPU:28, one launch (start us, length us, event | category | flops | bytes accessed | tf_op | source)
XLA Modules:
  0.0 387.4 jit_solution(15160892057513650524)
XLA Ops:
  8.6 1.8 pad_maximum_fusion.1
  15.8 43.9 %all-gather.6.cloned.1.call-done = bf16[2048,1792]{1,0:T(8,128)(2,1)} async-done(((bf16[128,1792]{1,0:T(8,128)(2,1)}), bf16[2048,1792]{1,0:T(8,128)(2,1)}) %all-gather.6.cloned.1.call-update) | async-done | bytes 7340048 | tf_op jit(solution)/shard_map/all_gather | solution.py:142
  59.8 1.9 slice-done
  61.6 3.0 copy.37
  64.7 4.5 %fusion.40 = f32[512,3,256]{0,2,1:T(8,128)S(1)} fusion(bf16[2048,3,256]{0,2,1:T(8,128)(2,1)} %bitcast.156, bf16[512,2048]{1,0:T(8,128)(2,1)} %param.14, f32[2048]{0:T(1024)S(1)} %copy-done.15, f32[512]{0:T(512)S(1)} %add_rsqrt_fusion, f32[512]{0:T(512)S(1)} %broadcast_multiply_fusion), kind=kOutput, calls=%fused_computation.61 | convolution fusion | flops 1615855616 | bytes 6828032 | tf_op jit(solution)/shard_map/td,dkh->tkh/dot_general | solution.py:144
  71.6 2.3 collective-permute-start
  73.9 38.7 %all-gather.8.cloned.1.call-done = bf16[2048,1280]{0,1:T(8,128)(2,1)} async-done(((bf16[128,1280]{0,1:T(8,128)(2,1)}), bf16[2048,1280]{0,1:T(8,128)(2,1)}) %all-gather.8.cloned.1.call-update) | async-done | bytes 5242896 | tf_op jit(solution)/shard_map/all_gather | solution.py:195
  112.6 14.3 %fusion.31 = f32[512,2048]{1,0:T(8,128)} fusion(bf16[2048,1280]{0,1:T(8,128)(2,1)} %all-gather.8.cloned.1.call-done, bf16[2048,1792]{1,0:T(8,128)(2,1)} %all-gather.6.cloned.1.call-done, bf16[512,2048]{1,0:T(8,128)(2,1)S(1)} %copy-done.1, f32[2048]{0:T(1024)S(1)} %copy-done.16, f32[512]{0:T(512)S(1)} %add_rsqrt_fusion, f32[512]{0:T(512)S(1)} %broadcast_multiply_fusion), kind=kOutput, calls=%fused_computation.51 | convolution fusion | flops 4334288896 | bytes 14692352 | tf_op jit(solution)/shard_map/tf,df->td/dot_general | solution.py:198
  131.0 1.3 copy-done.2
  133.1 74.4 %all-gather.4.cloned.1.call-done = bf16[128,128,2,256]{3,1,0,2:T(8,128)(2,1)} async-done(((bf16[8,128,2,256]{3,1,0,2:T(8,128)(2,1)}), bf16[128,128,2,256]{3,1,0,2:T(8,128)(2,1)}) %all-gather.4.cloned.1.call-update) | async-done | bytes 16777232 | tf_op jit(solution)/shard_map/all_gather | solution.py:182
  207.5 91.4 %while.20 = (s32[]{:T(128)}, f32[1,512]{1,0:T(1,128)S(1)}, f32[1,512]{1,0:T(1,128)S(1)}, f32[512,1,256]{0,2,1:T(8,128)}, s32[128]{0:T(128)S(1)}, /*index=5*/s32[...) while((s32[]{:T(128)}, f32[1,512]{1,0:T(1,128)S(1)}, ...), condition=%wide.region_11.12_spmd.clone, body=%wide.region_7.0_spmd.clone.sunk | while | flops 546315392 | bytes 11871218 | solution.py:111
  207.5 1.3 constant_dynamic-slice_fusion.3
  210.5 1.7 fusion.186
  215.3 2.7 fusion.186
  221.1 2.7 fusion.186
  226.8 2.7 fusion.186
  229.6 1.3 constant_dynamic-slice_fusion.3
  232.6 2.7 fusion.186
  238.4 2.7 fusion.186
  244.2 2.7 fusion.186
  249.9 2.7 fusion.186
  255.7 2.7 fusion.186
  261.5 2.7 fusion.186
  267.3 2.7 fusion.186
  273.0 2.7 fusion.186
  278.8 2.7 fusion.186
  284.6 2.7 fusion.186
  290.4 2.7 fusion.186
  296.2 2.7 fusion.186
  298.9 6.3 %add_convert_fusion = bf16[512,2048]{1,0:T(8,128)(2,1)} fusion(f32[512,2048]{1,0:T(8,128)} %fusion.31, bf16[2048,1280]{0,1:T(8,128)(2,1)} %all-gather.8.cloned.1.call-done, f32[512,1024]{1,0:T(8,128)} %copy-done.2, f32[512]{0:T(512)S(1)} %get-tuple-element.373, s32[1024]{0:T(1024)S(1)} %get-tuple-element.378, s32[1024]{0:T(1024)S(1)} %get-tuple-element.377, ...), kind=kOutput, calls=%fused_computation.55 | convolution fusion | flops 811204608 | bytes 10506240 | tf_op jit(solution)/shard_map/th,dh->td/dot_general | solution.py:196
  306.9 72.1 %reduce-scatter.2.cloned.1.call-done = bf16[512,256]{1,0:T(8,128)(2,1)} async-done(((bf16[512,2048]{1,0:T(8,128)(2,1)}), bf16[512,256]{1,0:T(8,128)(2,1)}) %reduce-scatter.2.cloned.1.call-update) | async-done | bytes 262160 | tf_op jit(solution)/shard_map/reduce_scatter | solution.py:199
  379.1 1.8 add_convert_fusion.1
  (243 shorter events, 61.6 us)
Async XLA Ops:
  7.2 3.3 copy-start.11
  7.2 3.3 copy-start.9
  7.2 4.1 %copy-start.6 = (bf16[8,128,2,256]{3,2,1,0:T(2,128)(2,1)S(1)}, bf16[8,128,2,256]{3,2,1,0:T(2,128)(2,1)}, u32[]{:S(2)}) copy-start(bf16[8,128,2,256]{3,2,1,0:T(2,128)(2,1)} %param.21) | copy-start | bytes 3145732
  7.2 52.6 %all-gather.6.cloned.1.call-start = ((), (), s32[]{:S(2)}) async-start(), calls=%async_computation.2 | async-start | bytes 7798784 | tf_op jit(solution)/shard_map/all_gather | solution.py:142
  10.4 2.2 copy-start.12
  10.4 102.2 %all-gather.8.cloned.1.call-start = ((), (), s32[]{:S(2)}) async-start(), calls=%async_computation.3 | async-start | bytes 5570560 | tf_op jit(solution)/shard_map/all_gather | solution.py:195
  10.5 2.9 copy-start.13
  10.5 2.9 copy-start.14
  11.2 3.2 copy-start
  11.3 196.2 %all-gather.4.cloned.1.call-start = ((), (), s32[]{:S(2)}) async-start(), calls=%async_computation.1 | async-start | bytes 17825792 | tf_op jit(solution)/shard_map/all_gather | solution.py:182
  12.5 366.6 %reduce-scatter.2.cloned.1.call-start = ((), (), s32[]{:S(2)}) async-start(), calls=%async_computation.4 | async-start | bytes 2359296 | tf_op jit(solution)/shard_map/reduce_scatter | solution.py:199
  59.8 1.9 slice-start
  61.6 3.0 copy-start.15
  69.2 43.4 %copy-start.1 = (bf16[512,2048]{1,0:T(8,128)(2,1)S(1)}, bf16[512,2048]{1,0:T(8,128)(2,1)}, u32[]{:S(2)}) copy-start(bf16[512,2048]{1,0:T(8,128)(2,1)} %param.14) | copy-start | bytes 6291460
  69.2 43.4 %copy-start.16 = (f32[2048]{0:T(1024)S(1)}, f32[2048]{0:T(1024)}, u32[]{:S(2)}) copy-start(f32[2048]{0:T(1024)} %param.16) | copy-start | bytes 24580
  71.6 57.3 %collective-permute-start = (bf16[512,2,256]{0,2,1:T(8,128)(2,1)}, bf16[512,2,256]{0,2,1:T(8,128)(2,1)}, u32[]{:S(2)}, u32[]{:S(2)}) collective-permute-start(bf16[512,2,256]{0,2,1:T(8,128)(2,1)} %pad_maximum_fusion), channel_id=1, source_target_pairs={{0,8},{8,16},{16,24},{24,32},{32,40},{40,48},{48,56},{56,64},{64,7... | collective-permute-start | bytes 1572872 | tf_op jit(solution)/shard_map/ppermute | solution.py:21
  126.9 1.9 copy-start.4
  126.9 3.1 copy-start.8
  131.0 76.4 %copy-start.17 = (s32[128]{0:T(128)S(1)}, s32[128]{0:T(128)}, u32[]{:S(2)}) copy-start(s32[128]{0:T(128)} %param.25) | copy-start | bytes 1540
  207.5 1.6 copy-start.10
  212.2 1.6 copy-start.10
  218.0 1.6 copy-start.10
  223.8 1.6 copy-start.10
  229.6 1.6 copy-start.10
  235.3 1.6 copy-start.10
  241.1 1.6 copy-start.10
  246.9 1.6 copy-start.10
  252.7 1.6 copy-start.10
  258.4 1.6 copy-start.10
  275.8 1.6 copy-start.10
  281.5 1.6 copy-start.10
  287.3 1.6 copy-start.10
  (7 other events, 9.6 us)
Sparse Core Ops, SparseCore 0:
  10.5 49.2 all-gather.5
  61.4 51.1 all-gather.7
  114.3 93.1 all-gather.3
  305.3 73.7 reduce-scatter.1

commit v2 on v1

--- a/solution.py
+++ b/solution.py
@@ -1,8 +1,11 @@
+import functools
 import math
 
 import jax
 import jax.numpy as jnp
 from jax import lax
+from jax.experimental import pallas as pl
+from jax.experimental.pallas import tpu as pltpu
 from jax.sharding import PartitionSpec as P
 
 HD = 256
@@ -109,6 +112,77 @@
         return combine(inner, partial_softmax(scores, visible, value_block))
 
     return lax.fori_loop(0, count // stride, advance, running)
+
+
+def attention_kernel(bounds_ref, q_ref, code_ref, pref_ref, win_ref, out_ref, m_ref, l_ref, acc_ref, *, steps):
+    step = pl.program_id(0)
+    width = q_ref.shape[1]
+
+    @pl.when(step == 0)
+    def _():
+        m_ref[...] = jnp.full(m_ref.shape, very_low, jnp.float32)
+        l_ref[...] = jnp.zeros(l_ref.shape, jnp.float32)
+        acc_ref[...] = jnp.zeros(acc_ref.shape, jnp.float32)
+
+    def fold(kv_ref, low, high):
+        keys = kv_ref[:, :width]
+        values = kv_ref[:, width:]
+        scores = lax.dot_general(
+            q_ref[...], keys, (((1,), (1,)), ((), ())), preferred_element_type=jnp.float32
+        )
+        code = code_ref[...]
+        visible = (code >= low) & (code < high)
+        peak_old = m_ref[...]
+        peak = jnp.maximum(
+            peak_old, jnp.max(jnp.where(visible, scores, very_low), axis=1, keepdims=True)
+        )
+        weights = jnp.where(visible, jnp.exp(scores - peak), 0.0)
+        scale = jnp.exp(peak_old - peak)
+        l_ref[...] = l_ref[...] * scale + jnp.sum(weights, axis=1, keepdims=True)
+        acc_ref[...] = acc_ref[...] * scale + jnp.dot(
+            weights.astype(jnp.bfloat16), values, preferred_element_type=jnp.float32
+        )
+        m_ref[...] = peak
+
+    @pl.when(step < steps)
+    def _():
+        fold(pref_ref, bounds_ref[:, 0:1], bounds_ref[:, 1:2])
+
+    @pl.when(step == steps)
+    def _():
+        fold(win_ref, bounds_ref[:, 2:3], bounds_ref[:, 3:4])
+        out_ref[...] = (acc_ref[...] / l_ref[...]).astype(out_ref.dtype)
+
+
+def attend(bounds, queries, codes, prefix_rows, window):
+    rows, width = queries.shape
+    block = window.shape[0]
+    steps = prefix_rows.shape[0] // block
+    keys_total = prefix_rows.shape[0] + block
+    return pl.pallas_call(
+        functools.partial(attention_kernel, steps=steps),
+        out_shape=jax.ShapeDtypeStruct((rows, width), jnp.bfloat16),
+        grid=(steps + 1,),
+        in_specs=[
+            pl.BlockSpec((rows, bounds.shape[1]), lambda i: (0, 0)),
+            pl.BlockSpec((rows, width), lambda i: (0, 0)),
+            pl.BlockSpec((1, block), lambda i: (0, i)),
+            pl.BlockSpec((block, 2 * width), lambda i: (jnp.minimum(i, steps - 1), 0)),
+            pl.BlockSpec((block, 2 * width), lambda i: (0, 0)),
+        ],
+        out_specs=pl.BlockSpec((rows, width), lambda i: (0, 0)),
+        scratch_shapes=[
+            pltpu.VMEM((rows, 1), jnp.float32),
+            pltpu.VMEM((rows, 1), jnp.float32),
+            pltpu.VMEM((rows, width), jnp.float32),
+        ],
+        compiler_params=pltpu.CompilerParams(dimension_semantics=("arbitrary",)),
+        cost_estimate=pl.CostEstimate(
+            flops=4 * rows * keys_total * width,
+            transcendentals=rows * keys_total,
+            bytes_accessed=2 * keys_total * 2 * width,
+        ),
+    )(bounds, queries, codes, prefix_rows, window)
 
 
 def body(
@@ -158,37 +232,35 @@
         rotary(projected[:, 1], local_position).astype(jnp.bfloat16).reshape(row_count, head_width)
     )
     values_flat = projected[:, 2].astype(jnp.bfloat16).reshape(row_count, head_width)
-    pair_rows = jnp.stack([keys_flat, values_flat], 1)
+    pair_rows = jnp.concatenate([keys_flat, values_flat], 1)
     previous = from_behind(pair_rows, "row", 1)
     window = jnp.concatenate([previous, pair_rows], 0)
-    window_ids = first_row - row_count + jnp.arange(2 * row_count, dtype=jnp.int32)
-    padded_request = jnp.concatenate([jnp.full((row_count,), -1, jnp.int32), request_all], 0)
-    window_request = lax.dynamic_slice_in_dim(padded_request, first_row, 2 * row_count, 0)
     token_ids = first_row + jnp.arange(row_count, dtype=jnp.int32)
-    visible = (window_request[None, :] == local_request[:, None]) & (
-        window_ids[None, :] <= token_ids[:, None]
-    )
-    window_keys = window[:, 0].reshape(2 * row_count, heads_here, HD)
-    window_values = window[:, 1].reshape(2 * row_count, heads_here, HD)
-    scores = jnp.einsum("qhe,khe->hqk", queries, window_keys, preferred_element_type=jnp.float32)
-    suffix_state = partial_softmax(scores, visible, window_values)
-    start_state = (
-        jnp.full((heads_here, row_count), very_low, jnp.float32),
-        jnp.zeros((heads_here, row_count), jnp.float32),
-        jnp.zeros((row_count, heads_here, HD), jnp.float32),
-    )
-    prefix_state = prefix_fold(
-        start_state,
-        lax.all_gather(prefix_cache, "row", axis=0, tiled=True),
-        queries,
-        local_group,
-        local_limit,
-        page_table,
-    )
-    final = combine(prefix_state, suffix_state)
-    attention = (
-        (final[2] / final[1].T[:, :, None]).astype(jnp.bfloat16).reshape(row_count, head_width)
-    )
+    local_begin = local_limit + token_ids - local_position
+    prefix_span = 2 * page_table.shape[0] // GROUPS * PAGE
+    bounds = jnp.stack(
+        [
+            local_group * prefix_span,
+            local_group * prefix_span + local_limit,
+            local_begin,
+            token_ids + 1,
+        ],
+        1,
+    )
+    per_prefix = page_table.shape[0] // GROUPS
+    slots = jnp.arange(page_table.shape[0], dtype=jnp.int32)
+    logical = jnp.sum(
+        slots[None, :] * (page_table[None, :] == slots[:, None]).astype(jnp.int32),
+        1,
+        dtype=jnp.int32,
+    )
+    slot_codes = (logical // per_prefix) * prefix_span + (logical % per_prefix) * PAGE
+    prefix_codes = (slot_codes[:, None] + jnp.arange(PAGE, dtype=jnp.int32)[None, :]).reshape(-1)
+    window_codes = first_row - row_count + jnp.arange(2 * row_count, dtype=jnp.int32)
+    codes = jnp.concatenate([prefix_codes, window_codes])[None, :]
+    cache_rows = prefix_cache.reshape(-1, 2 * head_width)
+    prefix_rows = lax.all_gather(cache_rows, "row", axis=0, tiled=True)
+    attention = attend(bounds, queries.reshape(row_count, head_width), codes, prefix_rows, window)
     activated = jax.nn.gelu(up_sum, approximate=False).astype(jnp.bfloat16)
     out_rows = w_out.shape[0]
     joined = jnp.concatenate([w_out.T, w_down.T], 1)

time: 392 us -> 337 us (0.86)
  matrix products: 77.4 us -> 23.6 us
  Pallas kernels: 0 us -> 37.6 us
  local copies, waits for them, and re-layouts: 33.8 us -> 9.43 us
  other arithmetic: 30 us -> 15.6 us
    dot_general x33 -> x0, matrix products: 52.4 us -> none  [the longest x16 42.5 us: partial_softmax(): jnp.einsum('hqk,khe->qhe', weights.astype(jnp.bfloat16), value_block, pre...]
    pallas_call x0 -> x1, Pallas kernels: none -> 37.6 us  [attend(): pl.pallas_call(functools.partial(attention_kernel, steps=steps), out_shap...]
    slice x18 -> x0, local copies, waits for them, and re-layouts: 21.1 us -> none  [the longest x16 21 us: advance(): value_block = block_rows[:, :, 1].reshape(stride * PAGE, heads_here, HD)]
    reduce_sum x33 -> x1, other arithmetic: 17.1 us -> 0.1 us  [body(): jnp.sum(slots[None, :] * (page_table[None, :] == slots[:, None]).astype(j...]
  transfers between devices with their start and end apart: 5 -> 5, of which waited for: 4 -> 4; matrix products, arithmetic and copies ran while one was open for 9% -> 11% of each run, Pallas kernels for 0% -> 0%
where the time goes in v2:
time: 337 us; the launch traced here: 333 us
  waiting for transfers between devices  230 us (68%)
  Pallas kernels  37.6 us (11%)
  matrix products  23.6 us (7%)
  other arithmetic  15.6 us (5%)
  between operations  14.1 us (4%)
  local copies, waits for them, and re-layouts  9.43 us (3%)
    all_gather x2, waiting for transfers between devices, body(): joined = lax.all_gather(joined, 'row', axis=0, tiled=True)  79.5 us
    all_gather x1, waiting for transfers between devices, body(): prefix_rows = lax.all_gather(cache_rows, 'row', axis=0, tiled=True)  77.7 us
    reduce_scatter x1, waiting for transfers between devices, body(): lax.psum_scatter(contribution.astype(jnp.bfloat16), 'col', scatter_dimens...  73 us
    pallas_call x1, Pallas kernels, attend(): pl.pallas_call(functools.partial(attention_kernel, steps=steps), out_shap...  37.6 us
    dot_general x1, matrix products, body(): jnp.einsum('tf,df->td', activated, joined[:, out_rows:], preferred_elemen...  14.5 us
  transfers between devices with their start and end apart: 5, of which 4 were waited for; matrix products, arithmetic and copies ran while one was open for 11% of the time, Pallas kernels for 0%

profile of v2, /device:TPU:28, one launch (start us, length us, event | category | flops | bytes accessed | tf_op | source)
XLA Modules:
  0.0 333.2 jit_solution(5603928448712270415)
XLA Ops:
  7.2 1.2 copy.34
  8.4 0.2 copy.35
  8.6 1.8 pad_maximum_fusion.1
  10.5 0.8 pad_maximum_fusion.2
  11.3 1.2 copy.40
  12.9 0.3 convert_reduce_fusion.1
  13.3 0.8 select_reduce_fusion.2
  14.3 0.9 copy.38.bounds_ref
  15.3 0.3 convert_reduce_fusion
  15.6 0.7 fusion.6
  16.3 1.8 fusion.75
  18.2 0.6 pad_add_fusion
  18.8 40.9 %all-gather.4.cloned.1.call-done = bf16[2048,1792]{1,0:T(8,128)(2,1)} async-done(((bf16[128,1792]{1,0:T(8,128)(2,1)}), bf16[2048,1792]{1,0:T(8,128)(2,1)}) %all-gather.4.cloned.1.call-update) | async-done | bytes 7340048 | tf_op jit(solution)/shard_map/all_gather | solution.py:216
  59.8 1.9 slice-done
  61.7 3.0 copy.36
  64.6 4.5 %fusion.31 = f32[512,3,1,256]{3,0,2,1:T(8,128)S(1)} fusion(bf16[2048,3,256]{0,2,1:T(8,128)(2,1)} %bitcast.48, bf16[512,2048]{1,0:T(8,128)(2,1)} %param.12, f32[2048]{0:T(1024)S(1)} %copy-done.11, f32[512]{0:T(512)S(1)} %add_rsqrt_fusion, f32[512]{0:T(512)S(1)} %broadcast_multiply_fusion), kind=kOutput, calls=%fused_computation.47 | convolution fusion | flops 1615855616 | bytes 6828032 | tf_op jit(solution)/shard_map/td,dkh->tkh/dot_general | solution.py:218
  69.4 0.2 slice_negate_fusion
  69.6 0.6 copy-done.3
  70.2 1.0 fusion.82
  71.2 1.0 pad_maximum_fusion
  72.2 2.4 collective-permute-start
  74.7 38.6 %all-gather.8.cloned.1.call-done = bf16[2048,1280]{0,1:T(8,128)(2,1)} async-done(((bf16[128,1280]{0,1:T(8,128)(2,1)}), bf16[2048,1280]{0,1:T(8,128)(2,1)}) %all-gather.8.cloned.1.call-update) | async-done | bytes 5242896 | tf_op jit(solution)/shard_map/all_gather | solution.py:267
  113.3 14.5 %fusion.7 = f32[512,2048]{1,0:T(8,128)} fusion(bf16[2048,1280]{0,1:T(8,128)(2,1)} %all-gather.8.cloned.1.call-done, bf16[2048,1792]{1,0:T(8,128)(2,1)} %all-gather.4.cloned.1.call-done, bf16[512,2048]{1,0:T(8,128)(2,1)S(1)} %copy-done.1, f32[2048]{0:T(1024)S(1)} %copy-done.12, f32[512]{0:T(512)S(1)} %add_rsqrt_fusion, f32[512]{0:T(512)S(1)} %broadcast_multiply_fusion), kind=kOutput, calls=%fused_computation.9 | convolution fusion | flops 4334288896 | bytes 14692352 | tf_op jit(solution)/shard_map/tf,df->td/dot_general | solution.py:270
  127.8 0.2 slice_bitcast_fusion.1
  128.0 0.9 fusion.74.q_ref
  128.9 2.2 maximum_maximum_fusion.win_ref
  131.1 77.7 %all-gather.6.cloned.1.call-done.pref_ref = bf16[16384,512]{1,0:T(8,128)(2,1)} async-done(((bf16[1024,512]{1,0:T(8,128)(2,1)}), bf16[16384,512]{1,0:T(8,128)(2,1)}) %all-gather.6.cloned.1.call-update) | async-done | bytes 16777232 | tf_op jit(solution)/shard_map/all_gather | solution.py:262
  208.8 37.6 %shard_map.139 = bf16[512,256]{1,0:T(8,128)(2,1)} custom-call(s32[512,4]{1,0:T(8,128)} %copy.38.bounds_ref, bf16[512,256]{1,0:T(8,128)(2,1)} %fusion.74.q_ref, s32[1,17408]{1,0:T(1,128)} %bitcast.52, bf16[16384,512]{1,0:T(8,128)(2,1)} %all-gather.6.cloned.1.call-done.pref_ref, bf16[1024,512]{1,0:T(8,128)(2,1)} %maximum_maximum_fusion.win_ref), custom_call_target="tpu_custom_call" | custom-call | flops 9126805504 | bytes 17825792 | tf_op jit(solution)/shard_map/pallas_call | solution.py:162
  246.4 4.7 %add_convert_fusion = bf16[512,2048]{1,0:T(8,128)(2,1)} fusion(f32[512,2048]{1,0:T(8,128)} %fusion.7, bf16[512,256]{1,0:T(8,128)(2,1)} %shard_map.139, bf16[2048,1280]{0,1:T(8,128)(2,1)} %all-gather.8.cloned.1.call-done), kind=kOutput, calls=%fused_computation.13 | convolution fusion | flops 538968064 | bytes 7602176 | tf_op jit(solution)/shard_map/th,dh->td/dot_general | solution.py:268
  251.0 0.9 pad_maximum_fusion.4
  251.9 73.0 %reduce-scatter.2.cloned.1.call-done = bf16[512,256]{1,0:T(8,128)(2,1)} async-done(((bf16[512,2048]{1,0:T(8,128)(2,1)}), bf16[512,256]{1,0:T(8,128)(2,1)}) %reduce-scatter.2.cloned.1.call-update) | async-done | bytes 262160 | tf_op jit(solution)/shard_map/reduce_scatter | solution.py:271
  324.9 1.7 add_convert_fusion.1
  (55 shorter events, 1.2 us)
Async XLA Ops:
  7.2 3.3 copy-start.7
  7.2 3.3 copy-start.6
  7.2 4.1 %copy-start.4 = (bf16[8,128,2,256]{3,2,1,0:T(2,128)(2,1)S(1)}, bf16[8,128,2,256]{3,2,1,0:T(2,128)(2,1)}, u32[]{:S(2)}) copy-start(bf16[8,128,2,256]{3,2,1,0:T(2,128)(2,1)} %param.19) | copy-start | bytes 3145732
  7.2 52.6 %all-gather.4.cloned.1.call-start = ((), (), s32[]{:S(2)}) async-start(), calls=%async_computation.1 | async-start | bytes 7798784 | tf_op jit(solution)/shard_map/all_gather | solution.py:216
  10.4 2.2 copy-start.8
  10.4 102.9 %all-gather.8.cloned.1.call-start = ((), (), s32[]{:S(2)}) async-start(), calls=%async_computation.3 | async-start | bytes 5570560 | tf_op jit(solution)/shard_map/all_gather | solution.py:267
  10.5 2.8 copy-start.9
  10.5 2.8 copy-start.10
  11.2 3.9 %copy-start.13 = (s32[128]{0:T(128)S(1)}, s32[128]{0:T(128)}, u32[]{:S(2)}) copy-start(s32[128]{0:T(128)} %param.23) | copy-start | bytes 1540
  11.2 4.0 %copy-start = (bf16[512,2048]{1,0:T(8,128)(2,1)S(1)}, bf16[512,2048]{1,0:T(8,128)(2,1)}, u32[]{:S(2)}) copy-start(bf16[512,2048]{1,0:T(8,128)(2,1)} %param.12) | copy-start | bytes 6291460
  11.3 197.5 %all-gather.6.cloned.1.call-start = ((), (), s32[]{:S(2)}) async-start(), calls=%async_computation.2 | async-start | bytes 17825792 | tf_op jit(solution)/shard_map/all_gather | solution.py:262
  12.6 312.4 %reduce-scatter.2.cloned.1.call-start = ((), (), s32[]{:S(2)}) async-start(), calls=%async_computation.4 | async-start | bytes 2359296 | tf_op jit(solution)/shard_map/reduce_scatter | solution.py:271
  59.8 1.9 slice-start
  61.7 3.0 copy-start.11
  69.1 59.7 %copy-start.2 = (bf16[512,256]{1,0:T(8,128)(2,1)}, bf16[512,256]{1,0:T(8,128)(2,1)S(1)}, u32[]{:S(2)}) copy-start(bf16[512,256]{1,0:T(8,128)(2,1)S(1)} %fusion.77) | copy-start | bytes 786436
  69.1 1.0 copy-start.3
  69.6 43.7 %copy-start.1 = (bf16[512,2048]{1,0:T(8,128)(2,1)S(1)}, bf16[512,2048]{1,0:T(8,128)(2,1)}, u32[]{:S(2)}) copy-start(bf16[512,2048]{1,0:T(8,128)(2,1)} %param.12) | copy-start | bytes 6291460
  69.6 43.7 %copy-start.12 = (f32[2048]{0:T(1024)S(1)}, f32[2048]{0:T(1024)}, u32[]{:S(2)}) copy-start(f32[2048]{0:T(1024)} %param.14) | copy-start | bytes 24580
  72.2 55.7 %copy-start.5 = (f32[512,64]{1,0:T(8,128)S(1)}, f32[512,64]{1,0:T(8,128)}, u32[]{:S(2)}) copy-start(f32[512,64]{1,0:T(8,128)} %get-tuple-element.9) | copy-start | bytes 393220
  72.2 56.7 %collective-permute-start = (bf16[512,512]{1,0:T(8,128)(2,1)}, bf16[512,512]{1,0:T(8,128)(2,1)}, u32[]{:S(2)}, u32[]{:S(2)}) collective-permute-start(bf16[512,512]{1,0:T(8,128)(2,1)} %pad_maximum_fusion), channel_id=1, source_target_pairs={{0,8},{8,16},{16,24},{24,32},{32,40},{40,48},{48,56},{56,64},{64,7... | collective-permute-start | bytes 1572872 | tf_op jit(solution)/shard_map/ppermute | solution.py:24
Sparse Core Ops, SparseCore 0:
  10.5 49.2 all-gather.3
  61.4 51.8 all-gather.7
  115.0 93.7 all-gather.5
  251.2 73.7 reduce-scatter.1
